TPU v7x, 32 devices: a whole 2x2x4 slice. The times are simulated.
32 devices in a mesh: parts: 2 (over y), row: 4 (over z), col: 4 (over x, core).
Axes of the slice: x: 2, y: 2, z: 4, core: 2. Of those that a mesh axis runs over, the one named last changes fastest.
Arguments:
- single: bfloat16 [8, 1024, 768], P(None, ('parts', 'row'), 'col'), parts along dimension 1, may hold values from -6 to 6
- pair_act: bfloat16 [1024, 512, 128], P(('parts', 'row'), 'col'), parts along dimension 0, may hold values from -6 to 6
- token_mask: int32 [1024], P(('parts', 'row')), parts along dimension 0, may hold values 0 or 1
- atom_feats: bfloat16 [8192, 128], P(('parts', 'row', 'col')), parts along dimension 0, may hold values from -6 to 6
- atom_token: int32 [8192], P(('parts', 'row', 'col')), parts along dimension 0, may hold values from 0 to 127, as said below
- atom_count: int32 [32], P(('parts', 'row', 'col')), parts along dimension 0, may hold values from 32 to 256, as said below
- atom_weight: bfloat16 [128, 768], P(None, 'col'), may hold values from -0.5 to 0.5
- bias_weight: bfloat16 [128, 2, 16], replicated, may hold values from -16 to 16
- qkvg_weight: bfloat16 [2, 4, 768, 768], P(None, None, 'col'), may hold values from -0.21875 to 0.21875
- out_weight: bfloat16 [2, 768, 768], P(None, 'col'), may hold values from -0.21875 to 0.21875
Outputs:
- updated: bfloat16 [8, 1024, 768], P(None, ('parts', 'row'), 'col'), parts along dimension 1
There are 2 independent parts, one for each index of `parts`. A program takes and returns all parts, laid end to end along the dimension named above; an argument that names none is the same for every part. Nothing has to cross between parts.
Inputs may be any that keep to these rules, and one draw needn't show every extreme that they name: `atom_token`: slots of a device hold atoms of the 128 tokens of that device's row block, numbered within the block; every token owns at least one live slot. The first atom_count slots of a device are live, the others are padding; in every draw some device has all 256 slots live.
All inputs are finite; a program needn't handle non-finite values. No bound on the sum of `token_mask` on one device may be relied on, other than what follows from the above.
Results may differ from a plain program's by a relative error of at most 0.014.
The roundings to bfloat16 on the way count: a program that leaves them out, or rounds other values in their place, can miss the bound.
Values may be sent and summed in bfloat16 or wider, within the bound.
A program may use at most 64 MiB of HBM per device.

v0:
```python
import math

import jax
import jax.numpy as jnp
from jax import lax
from jax.sharding import PartitionSpec as P

HEAD_DIM = 48
LAYERS = 2


EPS = 1e-05
MASKED = -1000000000.0
START_LOW = -1e30


def layer_norm(values):
    average = jnp.mean(values, axis=-1, keepdims=True)
    centered = values - average
    variance = jnp.mean(centered * centered, axis=-1, keepdims=True)
    return centered * lax.rsqrt(variance + EPS)


def per_device(
    single,
    pair_act,
    token_mask,
    atom_feats,
    atom_token,
    atom_count,
    atom_weight,
    bias_weight,
    qkvg_weight,
    out_weight,
):
    tok_rows = single.shape[1]
    sample_count = single.shape[0]
    slot_ids = jnp.arange(atom_feats.shape[0], dtype=jnp.int32)
    live_slots = slot_ids < atom_count[0]
    token_ids = jnp.arange(tok_rows, dtype=jnp.int32)
    owner_match = (token_ids[:, None] == atom_token[None, :]) & live_slots[None, :]
    owners = owner_match.astype(jnp.float32)
    counts = jnp.sum(owners, axis=1)
    atom_sums = jnp.dot(
        owner_match.astype(jnp.bfloat16), atom_feats, preferred_element_type=jnp.float32
    )
    sum_total, count_total = (
        lax.psum(atom_sums.astype(jnp.bfloat16), "col").astype(jnp.float32),
        lax.psum(counts[:, None].astype(jnp.bfloat16), "col").astype(jnp.float32),
    )
    pooled = (
        jnp.dot(sum_total, atom_weight.astype(jnp.float32), precision=lax.Precision.HIGHEST)
        / count_total
    )
    stream = (single.astype(jnp.float32) + pooled[None]).astype(jnp.bfloat16)
    pair_normed = layer_norm(pair_act.astype(jnp.float32)).astype(jnp.bfloat16)
    biases = jnp.einsum(
        "ijc,clh->lhij", pair_normed, bias_weight, preferred_element_type=jnp.float32
    ).astype(jnp.bfloat16)
    live_keys = (token_mask > 0).astype(jnp.bfloat16)[None, :]
    score_scale = 1.0 / math.sqrt(HEAD_DIM)
    for layer_idx in range(LAYERS):
        spread = lax.all_to_all(biases[layer_idx], "col", split_axis=0, concat_axis=2, tiled=True)
        gathered = lax.all_gather(stream, "col", axis=2, tiled=True)
        normed = layer_norm(gathered.astype(jnp.float32)).astype(jnp.bfloat16)
        projected = jnp.einsum(
            "std,fed->fste", normed, qkvg_weight[layer_idx], preferred_element_type=jnp.float32
        )
        head_width = projected.shape[3]
        heads_here = head_width // HEAD_DIM
        queries = (
            projected[0].astype(jnp.bfloat16).reshape(sample_count, tok_rows, heads_here, HEAD_DIM)
        )
        key_rows = projected[1].astype(jnp.bfloat16)
        value_rows = projected[2].astype(jnp.bfloat16)
        gating = jax.nn.sigmoid(projected[3])

        def attend(running, incoming, offset, queries=queries, spread=spread):
            top_old, summed_old, acc_old = running
            keys_in, values_in, live_in = incoming
            key_count = keys_in.shape[1]
            keys_heads = keys_in.reshape(sample_count, key_count, heads_here, HEAD_DIM)
            values_heads = values_in.reshape(sample_count, key_count, heads_here, HEAD_DIM)
            scores = (
                jnp.einsum(
                    "sqhd,skhd->shqk", queries, keys_heads, preferred_element_type=jnp.float32
                )
                * score_scale
            )
            scores = scores + spread.astype(jnp.float32)[None]
            scores = jnp.where(live_in[0][None, None, None, :] > 0, scores, MASKED)
            top_new = jnp.maximum(top_old, jnp.max(scores, axis=-1))
            exponent = jnp.exp(scores - top_new[..., None])
            summed_new = jnp.sum(exponent, axis=-1)
            weights = exponent.astype(jnp.bfloat16)
            acc_new = jnp.einsum(
                "shqk,skhd->shqd", weights, values_heads, preferred_element_type=jnp.float32
            )
            return (top_new, summed_new, acc_new)

        start_state = (
            jnp.full((sample_count, heads_here, tok_rows), START_LOW, jnp.float32),
            jnp.zeros((sample_count, heads_here, tok_rows), jnp.float32),
            jnp.zeros((sample_count, heads_here, tok_rows, HEAD_DIM), jnp.float32),
        )
        top_end, summed_end, acc_end = attend(
            start_state,
            (
                lax.all_gather(key_rows, "row", axis=1, tiled=True),
                lax.all_gather(value_rows, "row", axis=1, tiled=True),
                lax.all_gather(live_keys, "row", axis=1, tiled=True),
            ),
            jnp.int32(0),
        )
        attended = acc_end / summed_end[..., None]
        attended = attended.transpose(0, 2, 1, 3).reshape(sample_count, tok_rows, head_width)
        gated = (gating * attended).astype(jnp.bfloat16)
        out_rows = out_weight[layer_idx]

        def project(summed, incoming, offset, out_rows=out_rows):
            return jnp.einsum("std,ed->ste", incoming, out_rows, preferred_element_type=jnp.float32)

        zero_update = jnp.zeros((sample_count, tok_rows, out_rows.shape[0]), jnp.float32)
        update = project(
            zero_update, lax.all_gather(gated, "col", axis=2, tiled=True), jnp.int32(0)
        )
        stream = (stream.astype(jnp.float32) + update).astype(jnp.bfloat16)
    return stream


def solution(mesh):
    placed = (
        P(None, ("parts", "row"), "col"),
        P(("parts", "row"), "col", None),
        P(("parts", "row")),
        P(("parts", "row", "col"), None),
        P(("parts", "row", "col")),
        P(("parts", "row", "col")),
        P(None, "col"),
        P(),
        P(None, None, "col", None),
        P(None, "col", None),
    )
    return jax.shard_map(
        per_device,
        mesh=mesh,
        in_specs=placed,
        out_specs=P(None, ("parts", "row"), "col"),
        check_vma=False,
    )
```

profile of v0, /device:TPU:7, one launch (start us, length us, event | category | flops | bytes accessed | tf_op | source)
XLA Modules:
  0.0 295.6 jit_solution(7858886814213033118)
XLA Ops:
  7.4 0.8 convert_reduce_fusion.3
  8.2 0.8 convolution_convert_fusion
  9.0 11.0 %all-reduce = (bf16[128,128]{1,0:T(8,128)(2,1)S(1)}, bf16[128]{0:T(256)(128)(2,1)S(1)}) all-reduce(bf16[128,128]{1,0:T(8,128)(2,1)S(1)} %convolution_convert_fusion, bf16[128]{0:T(256)(128)(2,1)S(1)} %convert_reduce_fusion.3), channel_id=1, replica_groups=mesh['parts'=2,'row'=4,'col'=4] {'col'}, use_global_device_ids=true, to_apply=%region_0.0 | all-reduce | flops 16512 | bytes 66048 | tf_op jit(solution)/shard_map/psum | solution.py:48
  20.0 1.0 convolution_divide_fusion
  20.9 1.8 add_convert_fusion
  22.8 0.0 all-gather.15.cloned.1.call-update
  22.8 0.0 all-gather.23.cloned.1.call-start
  22.8 20.2 %all-gather.15.cloned.1.call-done = bf16[8,128,768]{1,2,0:T(8,128)(2,1)} async-done(((bf16[8,128,192]{1,2,0:T(8,128)(2,1)}), bf16[8,128,768]{1,2,0:T(8,128)(2,1)}) %all-gather.15.cloned.1.call-update) | async-done | bytes 1572880 | tf_op jit(solution)/shard_map/all_gather | solution.py:64
  43.0 1.7 convert_reduce_fusion.2
  44.8 1.8 fusion.25
  46.6 3.2 %fusion.87 = (bf16[4,8,128,192]{2,3,0,1:T(8,128)(2,1)S(1)}, f32[4,8,128,192]{2,3,0,1:T(8,128)}) fusion(bf16[2,4,192,768]{3,2,1,0:T(8,128)(2,1)S(1)} %copy-done.9, bf16[8,128,768]{1,2,0:T(8,128)(2,1)S(1)} %copy-done.4, f32[8,128]{1,0:T(8,128)S(1)} %add_rsqrt_fusion.2, f32[8,128]{1,0:T(8,128)S(1)} %broadcast_multiply_fusion.2), kind=kOutput, calls=%fused_computation.107 | convolution fusion | flops 1211891712 | bytes 7479296 | tf_op jit(solution)/shard_map/std,fed->fste/dot_general | solution.py:66
  49.9 1.0 fusion.86
  50.8 0.0 all-gather.23.cloned.1.call-update
  50.9 0.0 all-gather.25.cloned.1.call-start
  50.9 0.0 copy-start.3
  50.9 3.5 %convert_reduce_fusion = f32[128,128]{1,0:T(8,128)S(1)} fusion(bf16[128,128,128]{2,1,0:T(8,128)(2,1)} %param.11), kind=kLoop, calls=%fused_computation.1 | loop fusion | flops 4177920 | bytes 4259840 | tf_op jit(solution)/shard_map/reduce_sum | solution.py:18
  54.4 0.0 copy-start.10
  54.5 4.8 %fusion.2 = f32[128,128]{1,0:T(8,128)S(1)} fusion(bf16[128,128,128]{2,1,0:T(8,128)(2,1)S(1)} %copy-done.3, f32[128,128]{1,0:T(8,128)S(1)} %broadcast_multiply_fusion), kind=kLoop, calls=%fused_computation.4 | loop fusion | flops 8372224 | bytes 4325376 | tf_op jit(solution)/shard_map/reduce_sum | solution.py:20
  59.3 6.0 %fusion.38 = bf16[2,16,128,128]{3,1,0,2:T(8,128)(2,1)S(1)} fusion(bf16[128,128,128]{2,1,0:T(8,128)(2,1)S(1)} %copy-done.3, f32[128,128]{1,0:T(8,128)S(1)} %add_rsqrt_fusion, f32[128,128]{1,0:T(8,128)S(1)} %broadcast_multiply_fusion, bf16[128,2,16]{0,2,1:T(8,128)(2,1)S(1)} %copy-done.10), kind=kOutput, calls=%fused_computation.43 | convolution fusion | flops 143130624 | bytes 5382144 | tf_op jit(solution)/shard_map/ijc,clh->lhij/dot_general | solution.py:57
  65.3 0.0 copy-start.11
  65.3 0.0 all-gather.25.cloned.1.call-update
  65.3 0.2 slice_bitcast_fusion
  65.5 0.9 copy.26
  66.4 4.8 %all-to-all-start = ((bf16[16,128,128]{2,1,0:T(8,128)(2,1)}), bf16[16,128,128]{2,1,0:T(8,128)(2,1)S(1)}, u32[]{:S(2)}, u32[]{:S(2)}) async-start(bf16[16,128,128]{2,1,0:T(8,128)(2,1)} %copy.26), calls=%async_computation | async-start | bytes 1048576 | tf_op jit(solution)/shard_map/all_to_all | solution.py:63
  71.2 0.0 all-gather.17.cloned.1.call-start
  71.2 9.5 %all-gather.5 = bf16[4,1,128]{2,1,0:T(2,128)(2,1)S(1)} all-gather(bf16[1,1,128]{2,1,0:T(2,128)(2,1)S(1)} %fusion.80), channel_id=2, replica_groups=mesh['parts'=2,'row'=4,'col'=4] {'row'}, dimensions={0}, use_global_device_ids=true | all-gather | bytes 1280 | tf_op jit(solution)/shard_map/all_gather | solution.py:111
  80.7 0.0 all-to-all-done
  80.8 0.1 copy_bitcast_fusion.1
  80.9 8.6 %all-gather.23.cloned.1.call-done = bf16[1,8,512,192]{2,3,0,1:T(8,128)(2,1)} async-done(((bf16[1,8,128,192]{2,3,0,1:T(8,128)(2,1)}), bf16[1,8,512,192]{2,3,0,1:T(8,128)(2,1)}) %all-gather.23.cloned.1.call-update) | async-done | bytes 1572880 | tf_op jit(solution)/shard_map/all_gather | solution.py:109
  89.4 3.3 %fusion.8 = (f32[8,4,128]{2,1,0:T(4,128)S(1)}, f32[8,4,128,512]{3,2,1,0:T(8,128)S(1)}) fusion(f32[4,128,512]{2,1,0:T(8,128)S(1)} %copy_bitcast_fusion.1, pred[512]{0:T(512)(128)(4,1)S(1)} %bitcast.132, bf16[8,128,4,48]{1,3,2,0:T(8,128)(2,1)S(1)} %bitcast.126, bf16[8,512,4,48]{1,3,2,0:T(8,128)(2,1)} %bitcast.128), kind=kOutput, calls=%fused_computation.14 | convolution fusion | flops 209711104 | bytes 11420160 | tf_op jit(solution)/shard_map/sqhd,skhd->shqk/dot_general | solution.py:85
  92.7 0.0 copy-start.2
  92.8 3.2 %copy-done.2 = f32[8,4,128,512]{3,2,1,0:T(8,128)} copy-done((f32[8,4,128,512]{3,2,1,0:T(8,128)}, f32[8,4,128,512]{3,2,1,0:T(8,128)S(1)}, u32[]{:S(2)}) %copy-start.2) | copy-done | bytes 8388632
  96.0 2.3 fusion.4
  98.3 28.5 %all-gather.25.cloned.1.call-done = bf16[1,8,512,192]{2,3,0,1:T(8,128)(2,1)} async-done(((bf16[1,8,128,192]{2,3,0,1:T(8,128)(2,1)}), bf16[1,8,512,192]{2,3,0,1:T(8,128)(2,1)}) %all-gather.25.cloned.1.call-update) | async-done | bytes 1572880 | tf_op jit(solution)/shard_map/all_gather | solution.py:110
  126.8 6.3 %fusion.56 = f32[8,128,4,48]{1,3,2,0:T(8,128)S(1)} fusion(bf16[8,512,4,48]{1,3,2,0:T(8,128)(2,1)} %bitcast.138, f32[8,4,128,512]{3,2,1,0:T(8,128)} %copy-done.2, f32[8,4,128]{2,1,0:T(4,128)S(1)} %broadcast_maximum_fusion.1, f32[4,128,512]{2,1,0:T(8,128)S(1)} %copy_bitcast_fusion.1, pred[512]{0:T(512)(128)(4,1)S(1)} %bitcast.134, f32[8,128,4]{1,2,0:T(4,128)S(1)} %bitcast.131), kind=kOutput, calls=%fused_computation.61 | convolution fusion | flops 212008960 | bytes 11829760 | tf_op jit(solution)/shard_map/shqk,skhd->shqd/dot_general | solution.py:96
  133.2 2.2 fusion.69
  135.3 0.0 all-gather.17.cloned.1.call-update
  135.3 0.0 all-gather.19.cloned.1.call-start
  135.4 17.4 %all-gather.17.cloned.1.call-done = bf16[8,128,768]{1,2,0:T(8,128)(2,1)} async-done(((bf16[8,128,192]{1,2,0:T(8,128)(2,1)}), bf16[8,128,768]{1,2,0:T(8,128)(2,1)}) %all-gather.17.cloned.1.call-update) | async-done | bytes 1572880 | tf_op jit(solution)/shard_map/all_gather | solution.py:125
  152.7 2.6 fusion.47
  155.4 0.0 all-gather.19.cloned.1.call-update
  155.4 0.0 all-gather.27.cloned.1.call-start
  155.5 19.7 %all-gather.19.cloned.1.call-done = bf16[8,128,768]{1,2,0:T(8,128)(2,1)} async-done(((bf16[8,128,192]{1,2,0:T(8,128)(2,1)}), bf16[8,128,768]{1,2,0:T(8,128)(2,1)}) %all-gather.19.cloned.1.call-update) | async-done | bytes 1572880 | tf_op jit(solution)/shard_map/all_gather | solution.py:64
  175.2 1.7 convert_reduce_fusion.1
  176.9 1.8 fusion.23
  178.8 4.5 %fusion.88 = (bf16[4,8,128,192]{2,3,0,1:T(8,128)(2,1)S(1)}, f32[4,8,128,192]{2,3,0,1:T(8,128)}) fusion(bf16[2,4,192,768]{3,2,1,0:T(8,128)(2,1)} %param.18, bf16[8,128,768]{1,2,0:T(8,128)(2,1)S(1)} %copy-done.5, f32[8,128]{1,0:T(8,128)S(1)} %add_rsqrt_fusion.1, f32[8,128]{1,0:T(8,128)S(1)} %broadcast_multiply_fusion.1), kind=kOutput, calls=%fused_computation.108 | convolution fusion | flops 1211891712 | bytes 7479296 | tf_op jit(solution)/shard_map/std,fed->fste/dot_general | solution.py:66
  183.3 1.0 fusion.85
  184.3 0.0 all-gather.27.cloned.1.call-update
  184.3 0.0 all-gather.29.cloned.1.call-start
  184.3 0.7 all-gather.29.cloned.1.call-update
  185.0 0.0 all-gather.21.cloned.1.call-start
  185.1 0.1 copy.29
  185.2 10.3 %all_to_all.8 = bf16[16,128,128]{2,1,0:T(8,128)(2,1)S(1)} all-to-all(bf16[16,128,128]{2,1,0:T(8,128)(2,1)S(1)} %copy.29), channel_id=1, replica_groups=mesh['parts'=2,'row'=4,'col'=4] {'col'}, dimensions={0} | all-to-all | bytes 1048576 | tf_op jit(solution)/shard_map/all_to_all | solution.py:63
  195.5 0.1 copy_bitcast_fusion
  195.7 27.1 %all-gather.27.cloned.1.call-done = bf16[1,8,512,192]{2,3,0,1:T(8,128)(2,1)} async-done(((bf16[1,8,128,192]{2,3,0,1:T(8,128)(2,1)}), bf16[1,8,512,192]{2,3,0,1:T(8,128)(2,1)}) %all-gather.27.cloned.1.call-update) | async-done | bytes 1572880 | tf_op jit(solution)/shard_map/all_gather | solution.py:109
  222.8 3.3 %fusion.9 = (f32[8,4,128]{2,1,0:T(4,128)S(1)}, f32[8,4,128,512]{3,2,1,0:T(8,128)S(1)}) fusion(f32[4,128,512]{2,1,0:T(8,128)S(1)} %copy_bitcast_fusion, pred[512]{0:T(512)(128)(4,1)S(1)} %bitcast.135, bf16[8,128,4,48]{1,3,2,0:T(8,128)(2,1)S(1)} %bitcast.127, bf16[8,512,4,48]{1,3,2,0:T(8,128)(2,1)} %bitcast.129), kind=kOutput, calls=%fused_computation.15 | convolution fusion | flops 209711104 | bytes 11420160 | tf_op jit(solution)/shard_map/sqhd,skhd->shqk/dot_general | solution.py:85
  226.1 3.2 %copy-done.1 = f32[8,4,128,512]{3,2,1,0:T(8,128)} copy-done((f32[8,4,128,512]{3,2,1,0:T(8,128)}, f32[8,4,128,512]{3,2,1,0:T(8,128)S(1)}, u32[]{:S(2)}) %copy-start.1) | copy-done | bytes 8388632
  229.3 2.3 fusion.6
  231.6 28.6 %all-gather.29.cloned.1.call-done = bf16[1,8,512,192]{2,3,0,1:T(8,128)(2,1)} async-done(((bf16[1,8,128,192]{2,3,0,1:T(8,128)(2,1)}), bf16[1,8,512,192]{2,3,0,1:T(8,128)(2,1)}) %all-gather.29.cloned.1.call-update) | async-done | bytes 1572880 | tf_op jit(solution)/shard_map/all_gather | solution.py:110
  260.3 6.3 %fusion.53 = f32[8,128,4,48]{1,3,2,0:T(8,128)S(1)} fusion(bf16[8,512,4,48]{1,3,2,0:T(8,128)(2,1)} %bitcast.139, f32[8,4,128,512]{3,2,1,0:T(8,128)} %copy-done.1, f32[8,4,128]{2,1,0:T(4,128)S(1)} %broadcast_maximum_fusion, f32[4,128,512]{2,1,0:T(8,128)S(1)} %copy_bitcast_fusion, pred[512]{0:T(512)(128)(4,1)S(1)} %bitcast.137, f32[8,128,4]{1,2,0:T(4,128)S(1)} %bitcast.130), kind=kOutput, calls=%fused_computation.60 | convolution fusion | flops 212008960 | bytes 11829760 | tf_op jit(solution)/shard_map/shqk,skhd->shqd/dot_general | solution.py:96
  266.6 2.2 fusion.70
  268.7 0.0 all-gather.21.cloned.1.call-update
  268.7 17.4 %all-gather.21.cloned.1.call-done = bf16[8,128,768]{1,2,0:T(8,128)(2,1)} async-done(((bf16[8,128,192]{1,2,0:T(8,128)(2,1)}), bf16[8,128,768]{1,2,0:T(8,128)(2,1)}) %all-gather.21.cloned.1.call-update) | async-done | bytes 1572880 | tf_op jit(solution)/shard_map/all_gather | solution.py:125
  286.1 2.6 fusion.48
  (31 shorter events, 0.1 us)
Async XLA Ops:
  6.5 1.6 copy-start
  6.5 40.1 %copy-start.9 = (bf16[2,4,192,768]{3,2,1,0:T(8,128)(2,1)S(1)}, bf16[2,4,192,768]{3,2,1,0:T(8,128)(2,1)}, u32[]{:S(2)}) copy-start(bf16[2,4,192,768]{3,2,1,0:T(8,128)(2,1)} %param.18) | copy-start | bytes 7077892
  6.5 36.5 %all-gather.15.cloned.1.call-start = ((), (), s32[]{:S(2)}) async-start(), calls=%async_computation.2 | async-start | bytes 1966080 | tf_op jit(solution)/shard_map/all_gather | solution.py:64
  22.8 66.6 %all-gather.23.cloned.1.call-start = ((), (), s32[]{:S(2)}) async-start(), calls=%async_computation.6 | async-start | bytes 1966080 | tf_op jit(solution)/shard_map/all_gather | solution.py:109
  43.0 3.6 %copy-start.4 = (bf16[8,128,768]{1,2,0:T(8,128)(2,1)S(1)}, bf16[8,128,768]{1,2,0:T(8,128)(2,1)}, u32[]{:S(2)}) copy-start(bf16[8,128,768]{1,2,0:T(8,128)(2,1)} %all-gather.15.cloned.1.call-done) | copy-start | bytes 4718596
  50.9 76.0 %all-gather.25.cloned.1.call-start = ((), (), s32[]{:S(2)}) async-start(), calls=%async_computation.7 | async-start | bytes 1966080 | tf_op jit(solution)/shard_map/all_gather | solution.py:110
  50.9 3.6 %copy-start.3 = (bf16[128,128,128]{2,1,0:T(8,128)(2,1)S(1)}, bf16[128,128,128]{2,1,0:T(8,128)(2,1)}, u32[]{:S(2)}) copy-start(bf16[128,128,128]{2,1,0:T(8,128)(2,1)} %param.11) | copy-start | bytes 12582916
  54.4 4.8 %copy-start.10 = (bf16[128,2,16]{0,2,1:T(8,128)(2,1)S(1)}, bf16[128,2,16]{0,2,1:T(8,128)(2,1)}, u32[]{:S(2)}) copy-start(bf16[128,2,16]{0,2,1:T(8,128)(2,1)} %param.17) | copy-start | bytes 24580
  65.3 6.0 %copy-start.11 = (s32[128]{0:T(128)S(1)}, s32[128]{0:T(128)}, u32[]{:S(2)}) copy-start(s32[128]{0:T(128)} %param.12) | copy-start | bytes 1540
  66.4 14.3 %all-to-all-start = ((bf16[16,128,128]{2,1,0:T(8,128)(2,1)}), bf16[16,128,128]{2,1,0:T(8,128)(2,1)S(1)}, u32[]{:S(2)}, u32[]{:S(2)}) async-start(bf16[16,128,128]{2,1,0:T(8,128)(2,1)} %copy.26), calls=%async_computation | async-start | bytes 1048576 | tf_op jit(solution)/shard_map/all_to_all | solution.py:63
  71.2 81.5 %all-gather.17.cloned.1.call-start = ((), (), s32[]{:S(2)}) async-start(), calls=%async_computation.3 | async-start | bytes 1966080 | tf_op jit(solution)/shard_map/all_gather | solution.py:125
  92.7 3.2 %copy-start.2 = (f32[8,4,128,512]{3,2,1,0:T(8,128)}, f32[8,4,128,512]{3,2,1,0:T(8,128)S(1)}, u32[]{:S(2)}) copy-start(f32[8,4,128,512]{3,2,1,0:T(8,128)S(1)} %get-tuple-element.18) | copy-start | bytes 25165828
  126.8 25.9 %copy-start.6 = (bf16[8,128,192]{1,2,0:T(8,128)(2,1)S(1)}, bf16[8,128,192]{1,2,0:T(8,128)(2,1)}, u32[]{:S(2)}) copy-start(bf16[8,128,192]{1,2,0:T(8,128)(2,1)} %add_convert_fusion) | copy-start | bytes 1179652
  126.8 25.9 %copy-start.8 = (bf16[2,192,768]{2,1,0:T(8,128)(2,1)S(1)}, bf16[2,192,768]{2,1,0:T(8,128)(2,1)}, u32[]{:S(2)}) copy-start(bf16[2,192,768]{2,1,0:T(8,128)(2,1)} %param.19) | copy-start | bytes 1769476
  135.3 39.9 %all-gather.19.cloned.1.call-start = ((), (), s32[]{:S(2)}) async-start(), calls=%async_computation.4 | async-start | bytes 1966080 | tf_op jit(solution)/shard_map/all_gather | solution.py:64
  155.4 67.4 %all-gather.27.cloned.1.call-start = ((), (), s32[]{:S(2)}) async-start(), calls=%async_computation.8 | async-start | bytes 1966080 | tf_op jit(solution)/shard_map/all_gather | solution.py:109
  175.2 3.6 %copy-start.5 = (bf16[8,128,768]{1,2,0:T(8,128)(2,1)S(1)}, bf16[8,128,768]{1,2,0:T(8,128)(2,1)}, u32[]{:S(2)}) copy-start(bf16[8,128,768]{1,2,0:T(8,128)(2,1)} %all-gather.19.cloned.1.call-done) | copy-start | bytes 4718596
  184.3 76.0 %all-gather.29.cloned.1.call-start = ((), (), s32[]{:S(2)}) async-start(), calls=%async_computation.9 | async-start | bytes 1966080 | tf_op jit(solution)/shard_map/all_gather | solution.py:110
  185.0 101.1 %all-gather.21.cloned.1.call-start = ((), (), s32[]{:S(2)}) async-start(), calls=%async_computation.5 | async-start | bytes 1966080 | tf_op jit(solution)/shard_map/all_gather | solution.py:125
  226.1 3.2 %copy-start.1 = (f32[8,4,128,512]{3,2,1,0:T(8,128)}, f32[8,4,128,512]{3,2,1,0:T(8,128)S(1)}, u32[]{:S(2)}) copy-start(f32[8,4,128,512]{3,2,1,0:T(8,128)S(1)} %get-tuple-element.22) | copy-start | bytes 25165828
  260.3 25.9 %copy-start.7 = (bf16[8,128,192]{1,2,0:T(8,128)(2,1)S(1)}, bf16[8,128,192]{1,2,0:T(8,128)(2,1)}, u32[]{:S(2)}) copy-start(bf16[8,128,192]{1,2,0:T(8,128)(2,1)} %fusion.47) | copy-start | bytes 1179652
Sparse Core Ops, SparseCore 0:
  22.9 20.0 all-gather.14
  51.0 38.4 all-gather.22
  91.0 35.7 all-gather.24
  135.5 17.2 all-gather.16
  155.5 19.6 all-gather.18
  184.4 38.2 all-gather.26
  224.3 35.8 all-gather.28
  268.9 17.2 all-gather.20
where the time goes:
time: 298 us; the launch traced here: 296 us
  waiting for transfers between devices  168 us (56%)
  matrix products  39.9 us (13%)
  blocking collectives  30.7 us (10%)
  other arithmetic  27.3 us (9%)
  between operations  14.6 us (5%)
  local copies, waits for them, and re-layouts  9.73 us (3%)
  starting transfers between devices  5.05 us (2%)
    all_gather x2, waiting for transfers between devices, per_device(): lax.all_gather(value_rows, 'row', axis=1, tiled=True)  57.1 us
    all_gather x2, waiting for transfers between devices, per_device(): gathered = lax.all_gather(stream, 'col', axis=2, tiled=True)  39.9 us
    all_gather x2, waiting for transfers between devices, per_device(): lax.all_gather(key_rows, 'row', axis=1, tiled=True)  35.7 us
    all_gather x2, waiting for transfers between devices, per_device(): lax.all_gather(gated, 'col', axis=2, tiled=True)  34.8 us
    dot_general x2, matrix products, attend(): jnp.einsum('shqk,skhd->shqd', weights, values_heads, preferred_element_ty...  12.6 us
    psum x1, blocking collectives, per_device(): lax.psum(atom_sums.astype(jnp.bfloat16), 'col').astype(jnp.float32)  11 us
    all_to_all x1, blocking collectives, per_device(): lax.all_to_all(biases[layer_idx], 'col', split_axis=0, concat_axis=2, til...  10.3 us
    all_gather x1, blocking collectives, per_device(): lax.all_gather(live_keys, 'row', axis=1, tiled=True)  9.47 us
  transfers between devices with their start and end apart: 9, of which 8 were waited for; matrix products, arithmetic and copies ran while one was open for 9% of the time, Pallas kernels for 0%

commit v1 on v0

--- a/solution.py
+++ b/solution.py
@@ -3,6 +3,8 @@
 import jax
 import jax.numpy as jnp
 from jax import lax
+from jax.experimental import pallas as pl
+from jax.experimental.pallas import tpu as pltpu
 from jax.sharding import PartitionSpec as P
 
 HEAD_DIM = 48
@@ -128,7 +130,611 @@
     return stream
 
 
+MESH = pl.DeviceIdType.MESH
+NT = (((1,), (1,)), ((), ()))
+
+
+def remote(src, dst, send_sem, recv_sem, row, col):
+    return pltpu.make_async_remote_copy(
+        src_ref=src,
+        dst_ref=dst,
+        send_sem=send_sem,
+        recv_sem=recv_sem,
+        device_id={"row": row, "col": col},
+        device_id_type=MESH,
+    )
+
+
+def fused(
+    rows,
+    cols,
+    bias,
+    single,
+    feats,
+    slot_token,
+    slot_count,
+    atom_weight,
+    mask,
+    qkvg,
+    out_w,
+    out,
+    spread,
+    normed,
+    out_full,
+    stream,
+    parts_buf,
+    stream_send,
+    stream_recv,
+    mask_buf,
+    queries,
+    keys,
+    values,
+    gates,
+    gated_send,
+    gated_recv,
+    final_send,
+    part_sems,
+    mask_sems,
+    a2a_sems,
+    ring_sems,
+    out_w_sems,
+    in_sems,
+    ag_sems,
+    gated_sems,
+    end_sems,
+):
+    r = lax.axis_index("row")
+    c = lax.axis_index("col")
+    own = single.shape[0] // rows
+    tokens = single.shape[1]
+    width = single.shape[2]
+    heads = width // HEAD_DIM
+    depth = rows * tokens
+    sibling = c + 1 - 2 * lax.rem(c, 2)
+    across = lax.rem(c + 2, cols)
+    far = lax.rem(sibling + 2, cols)
+    on_diag = r == c
+
+    barrier = pltpu.get_barrier_semaphore()
+    for dr in range(rows):
+        for dc in range(cols):
+            if dr or dc:
+                pl.semaphore_signal(
+                    barrier,
+                    inc=1,
+                    device_id={"row": lax.rem(r + dr, rows), "col": lax.rem(c + dc, cols)},
+                    device_id_type=MESH,
+                )
+    pl.semaphore_wait(barrier, rows * cols - 1)
+
+    sent = []
+
+    def col_of(d):
+        return lax.rem(c + d, cols)
+
+    def bias_exchange(l):
+        for d in range(1, cols):
+            to = col_of(d)
+            desc = remote(
+                bias.at[l, to],
+                spread.at[l, r, c],
+                a2a_sems.at[0, l, d],
+                a2a_sems.at[1, l, d],
+                r,
+                to,
+            )
+            desc.start()
+            sent.append(desc)
+        spread[l, r, c] = bias[l, c]
+
+    def bias_exchange_wait(l):
+        for d in range(1, cols):
+            frm = col_of(cols - d)
+            remote(
+                bias.at[l, frm],
+                spread.at[l, r, frm],
+                a2a_sems.at[0, l, d],
+                a2a_sems.at[1, l, d],
+                r,
+                frm,
+            ).wait_recv()
+
+    def ring_desc(l, right, step, block):
+        side = 0 if right else 1
+        to = r + 1 if right else r - 1
+        return remote(
+            spread.at[l, block],
+            spread.at[l, block],
+            ring_sems.at[0, l, side, step],
+            ring_sems.at[1, l, side, step],
+            to,
+            c,
+        )
+
+    def ring_send(l, step):
+        @pl.when((r + 1 < rows) & (r - step >= 0))
+        def _():
+            ring_desc(l, True, step, r - step).start()
+
+        @pl.when((r - 1 >= 0) & (r + step < rows))
+        def _():
+            ring_desc(l, False, step, r + step).start()
+
+    def ring_sent(l, step):
+        @pl.when((r + 1 < rows) & (r - step >= 0))
+        def _():
+            ring_desc(l, True, step, r - step).wait_send()
+
+        @pl.when((r - 1 >= 0) & (r + step < rows))
+        def _():
+            ring_desc(l, False, step, r + step).wait_send()
+
+    def advance(l, step):
+        @pl.when(r - 1 - step >= 0)
+        def _():
+            block = r - 1 - step
+            remote(
+                spread.at[l, block],
+                spread.at[l, block],
+                ring_sems.at[0, l, 0, step],
+                ring_sems.at[1, l, 0, step],
+                r - 1,
+                c,
+            ).wait_recv()
+
+        @pl.when((r - 1 - step >= 0) & (r + 1 < rows) & (step + 1 < rows - 1))
+        def _():
+            ring_desc(l, True, step + 1, r - step - 1).start()
+
+        @pl.when(r + 1 + step < rows)
+        def _():
+            block = r + 1 + step
+            remote(
+                spread.at[l, block],
+                spread.at[l, block],
+                ring_sems.at[0, l, 1, step],
+                ring_sems.at[1, l, 1, step],
+                r + 1,
+                c,
+            ).wait_recv()
+
+        @pl.when((r + 1 + step < rows) & (r - 1 >= 0) & (step + 1 < rows - 1))
+        def _():
+            ring_desc(l, False, step + 1, r + step + 1).start()
+
+    for d in range(1, rows):
+        to = lax.rem(r + d, rows)
+        desc = remote(mask, mask_buf.at[r], mask_sems.at[0, d], mask_sems.at[1, d], to, c)
+        desc.start()
+        sent.append(desc)
+    mask_buf[r] = mask[...]
+
+    slots = feats.shape[0]
+    token_ids = lax.broadcasted_iota(jnp.int32, (tokens, slots), 0)
+    slot_ids = lax.broadcasted_iota(jnp.int32, (tokens, slots), 1)
+    match = (token_ids == slot_token[...]) & (slot_ids < slot_count[...])
+    owners = jnp.where(match, 1.0, 0.0).astype(jnp.bfloat16)
+    parts_buf[c, 0:tokens] = jnp.dot(
+        owners, feats[...], preferred_element_type=jnp.float32
+    ).astype(jnp.bfloat16)
+    parts_buf[c, tokens : tokens + 16] = lax.dot_general(
+        jnp.ones((16, slots), jnp.bfloat16), owners, NT, preferred_element_type=jnp.float32
+    ).astype(jnp.bfloat16)
+    for d in range(1, cols):
+        desc = remote(
+            parts_buf.at[c], parts_buf.at[c], part_sems.at[0, d], part_sems.at[1, d], r, col_of(d)
+        )
+        desc.start()
+        sent.append(desc)
+    bias_exchange(0)
+    for d in range(1, cols):
+        frm = col_of(cols - d)
+        remote(
+            parts_buf.at[frm], parts_buf.at[frm], part_sems.at[0, d], part_sems.at[1, d], r, frm
+        ).wait_recv()
+    total = jnp.zeros((tokens, width), jnp.float32)
+    count_row = jnp.zeros((1, tokens), jnp.float32)
+    for k in range(cols):
+        total = total + jnp.dot(
+            parts_buf[k, 0:tokens], atom_weight[...], preferred_element_type=jnp.float32
+        )
+        count_row = count_row + parts_buf[k, tokens : tokens + 16].astype(jnp.float32)[0:1]
+    square = (
+        lax.broadcasted_iota(jnp.int32, (tokens, tokens), 0)
+        == lax.broadcasted_iota(jnp.int32, (tokens, tokens), 1)
+    )
+    count_col = jnp.sum(jnp.where(square, count_row, 0.0), axis=1, keepdims=True)
+    pooled = total / count_col
+    for s in range(single.shape[0]):
+        stream_send[s] = (single[s].astype(jnp.float32) + pooled).astype(jnp.bfloat16)
+    for d in range(rows):
+        to = lax.rem(r + d, rows)
+        piece = stream_send.at[pl.ds(to * own, own)]
+        if d == 0:
+
+            @pl.when(on_diag)
+            def _():
+                stream_recv[c] = stream_send[pl.ds(r * own, own)]
+
+            @pl.when(jnp.logical_not(on_diag))
+            def _(piece=piece, to=to):
+                remote(piece, stream_recv.at[c], in_sems.at[0, 0], in_sems.at[1, c], to, r).start()
+
+        else:
+            desc = remote(piece, stream_recv.at[c], in_sems.at[0, d], in_sems.at[1, c], to, r)
+            desc.start()
+            sent.append(desc)
+
+    bias_exchange_wait(0)
+    ring_send(0, 0)
+    bias_exchange(1)
+
+    for kind, to in ((0, sibling), (1, across)):
+        desc = remote(
+            out_w, out_full.at[c], out_w_sems.at[0, kind], out_w_sems.at[1, kind], r, to
+        )
+        desc.start()
+        sent.append(desc)
+    out_full[c] = out_w[...]
+
+    for f in range(cols):
+
+        @pl.when(jnp.logical_not(on_diag & (c == f)))
+        def _(f=f):
+            remote(
+                stream_recv.at[f],
+                stream_recv.at[f],
+                in_sems.at[0, 0],
+                in_sems.at[1, f],
+                c,
+                f,
+            ).wait_recv()
+
+    def send_normed(l, s, here):
+        average = jnp.mean(here, axis=-1, keepdims=True)
+        centered = here - average
+        variance = jnp.mean(centered * centered, axis=-1, keepdims=True)
+        normed[l, s, c] = (centered * lax.rsqrt(variance + EPS)).astype(jnp.bfloat16)
+        for kind, to in ((0, sibling), (1, across)):
+            desc = remote(
+                normed.at[l, s, c],
+                normed.at[l, s, c],
+                ag_sems.at[0, l, s, kind],
+                ag_sems.at[1, l, s, kind],
+                r,
+                to,
+            )
+            desc.start()
+            sent.append(desc)
+
+    def forward_normed(l, s):
+        remote(
+            normed.at[l, s, across],
+            normed.at[l, s, across],
+            ag_sems.at[0, l, s, 1],
+            ag_sems.at[1, l, s, 1],
+            r,
+            across,
+        ).wait_recv()
+        desc = remote(
+            normed.at[l, s, across],
+            normed.at[l, s, across],
+            ag_sems.at[0, l, s, 2],
+            ag_sems.at[1, l, s, 2],
+            r,
+            sibling,
+        )
+        desc.start()
+        sent.append(desc)
+
+    def project(l, s):
+        for kind, block in ((0, sibling), (2, far)):
+            remote(
+                normed.at[l, s, block],
+                normed.at[l, s, block],
+                ag_sems.at[0, l, s, kind],
+                ag_sems.at[1, l, s, kind],
+                r,
+                sibling,
+            ).wait_recv()
+        here = normed[l, s].reshape(depth, normed.shape[-1])
+        for f, target in enumerate((queries, keys, values)):
+            target[s] = lax.dot_general(
+                here, qkvg[l, f], NT, preferred_element_type=jnp.float32
+            ).astype(jnp.bfloat16)
+        gates[s] = jax.nn.sigmoid(
+            lax.dot_general(here, qkvg[l, 3], NT, preferred_element_type=jnp.float32)
+        )
+
+    score_scale = 1.0 / math.sqrt(HEAD_DIM)
+
+    def attend(l, block):
+        live = jnp.concatenate([mask_buf[k][0:1] for k in range(rows)], axis=1) > 0
+        lane_head = lax.broadcasted_iota(jnp.int32, (tokens, width), 1)
+
+        def one_sample(s, carry):
+            rows_at = pl.ds(pl.multiple_of(block * tokens, tokens), tokens)
+            query = queries[s, rows_at, :]
+            attended = jnp.zeros((tokens, width), jnp.float32)
+            for h in range(heads):
+                mine = (lane_head >= h * HEAD_DIM) & (lane_head < (h + 1) * HEAD_DIM)
+                masked = jnp.where(mine, query.astype(jnp.float32), 0.0).astype(jnp.bfloat16)
+                scores = (
+                    lax.dot_general(masked, keys[s], NT, preferred_element_type=jnp.float32)
+                    * score_scale
+                )
+                head_bias = jnp.concatenate([spread[l, block, k, h] for k in range(cols)], axis=1)
+                scores = scores + head_bias.astype(jnp.float32)
+                scores = jnp.where(live, scores, MASKED)
+                highest = jnp.max(scores, axis=-1, keepdims=True)
+                exponent = jnp.exp(scores - highest)
+                summed = jnp.sum(exponent, axis=-1, keepdims=True)
+                mixed = jnp.dot(
+                    exponent.astype(jnp.bfloat16), values[s], preferred_element_type=jnp.float32
+                )
+                attended = jnp.where(mine, mixed * (1.0 / summed), attended)
+            gated_send[l, block, s] = (gates[s, rows_at, :] * attended).astype(jnp.bfloat16)
+            return carry
+
+        lax.fori_loop(0, own, one_sample, 0)
+
+        gap = lax.rem(block - c + cols, cols)
+
+        @pl.when(block != c)
+        def _():
+            remote(
+                gated_send.at[l, block],
+                gated_recv.at[l, c],
+                gated_sems.at[0, l, gap],
+                gated_sems.at[1, l, gap],
+                r,
+                block,
+            ).start()
+
+        @pl.when(block == c)
+        def _():
+            gated_recv[l, c] = gated_send[l, block]
+
+    def gated_wait(l):
+        for d in range(1, cols):
+            frm = col_of(cols - d)
+            remote(
+                gated_send.at[l, frm],
+                gated_recv.at[l, frm],
+                gated_sems.at[0, l, d],
+                gated_sems.at[1, l, d],
+                r,
+                frm,
+            ).wait_recv()
+
+    for d in range(1, rows):
+        frm = lax.rem(r + rows - d, rows)
+        remote(
+            mask, mask_buf.at[frm], mask_sems.at[0, d], mask_sems.at[1, d], frm, c
+        ).wait_recv()
+
+    for s in range(own):
+        here = jnp.concatenate([stream_recv[f, s].astype(jnp.float32) for f in range(cols)], axis=1)
+        stream[s] = here
+        send_normed(0, s, here)
+
+    for l in range(LAYERS):
+        if l > 0:
+            advance(l, 0)
+        for s in range(own):
+            forward_normed(l, s)
+        for s in range(own):
+            project(l, s)
+        if l == 0:
+            advance(l, 0)
+            remote(
+                out_w, out_full.at[across], out_w_sems.at[0, 1], out_w_sems.at[1, 1], r, across
+            ).wait_recv()
+            desc = remote(
+                out_full.at[across],
+                out_full.at[across],
+                out_w_sems.at[0, 2],
+                out_w_sems.at[1, 2],
+                r,
+                sibling,
+            )
+            desc.start()
+            sent.append(desc)
+
+        def ring_round(t, carry, l=l):
+            def side(k, inner):
+                block = r - t + 2 * t * k
+
+                @pl.when((block >= 0) & (block < rows) & (k <= t))
+                def _():
+                    attend(l, block)
+
+                return inner
+
+            lax.fori_loop(0, 2, side, 0)
+
+            @pl.when((t >= 1) & (t < rows - 1))
+            def _():
+                advance(l, t)
+
+            return carry
+
+        lax.fori_loop(0, rows, ring_round, 0)
+        if l + 1 < LAYERS:
+            bias_exchange_wait(l + 1)
+            ring_send(l + 1, 0)
+        if l == 0:
+            for kind, block in ((0, sibling), (2, far)):
+                remote(
+                    out_w,
+                    out_full.at[block],
+                    out_w_sems.at[0, kind],
+                    out_w_sems.at[1, kind],
+                    r,
+                    sibling,
+                ).wait_recv()
+        gated_wait(l)
+        for s in range(own):
+            joined = jnp.concatenate(
+                [gated_recv[l, k, s].astype(jnp.float32) for k in range(cols)], axis=1
+            ).astype(jnp.bfloat16)
+            weight = jnp.concatenate([out_full[k, l] for k in range(cols)], axis=0)
+            here = stream[s] + lax.dot_general(
+                joined, weight, NT, preferred_element_type=jnp.float32
+            )
+            rounded = here.astype(jnp.bfloat16)
+            here = rounded.astype(jnp.float32)
+            if l + 1 < LAYERS:
+                stream[s] = here
+                send_normed(l + 1, s, here)
+            else:
+                for f in range(cols):
+                    final_send[f, s] = here[:, f * width : (f + 1) * width].astype(jnp.bfloat16)
+
+    place = pl.ds(r * own, own)
+
+    def end_desc(f):
+        return remote(final_send.at[f], out.at[place], end_sems.at[0, f], end_sems.at[1, r], c, f)
+
+    for f in range(cols):
+        stays = on_diag & (c == f)
+
+        @pl.when(stays)
+        def _(f=f):
+            out[place] = final_send[f]
+
+        @pl.when(jnp.logical_not(stays))
+        def _(f=f):
+            end_desc(f).start()
+
+    for k in range(rows):
+
+        @pl.when(jnp.logical_not(on_diag & (r == k)))
+        def _(k=k):
+            remote(
+                final_send.at[0],
+                out.at[pl.ds(k * own, own)],
+                end_sems.at[0, 0],
+                end_sems.at[1, k],
+                k,
+                r,
+            ).wait_recv()
+
+    for f in range(cols):
+
+        @pl.when(jnp.logical_not(on_diag & (c == f)))
+        def _(f=f):
+            end_desc(f).wait_send()
+
+    for desc in sent:
+        desc.wait_send()
+
+    @pl.when(jnp.logical_not(on_diag))
+    def _():
+        remote(
+            stream_send.at[pl.ds(r * own, own)],
+            stream_recv.at[c],
+            in_sems.at[0, 0],
+            in_sems.at[1, c],
+            r,
+            r,
+        ).wait_send()
+
+    for l in range(LAYERS):
+        for step in range(rows - 1):
+            ring_sent(l, step)
+        for d in range(1, cols):
+            to = col_of(d)
+            remote(
+                gated_send.at[l, to],
+                gated_recv.at[l, c],
+                gated_sems.at[0, l, d],
+                gated_sems.at[1, l, d],
+                r,
+                to,
+            ).wait_send()
+
+
+def per_device_fused(
+    rows,
+    cols,
+    single,
+    pair_act,
+    token_mask,
+    atom_feats,
+    atom_token,
+    atom_count,
+    atom_weight,
+    bias_weight,
+    qkvg_weight,
+    out_weight,
+):
+    samples, tokens, width = single.shape
+    own = samples // rows
+    depth = rows * tokens
+    heads = width // HEAD_DIM
+    full = width * cols
+    chans = atom_feats.shape[1]
+    slots = atom_feats.shape[0]
+    pair_normed = layer_norm(pair_act.astype(jnp.float32)).astype(jnp.bfloat16)
+    biases = (
+        jnp.einsum("ijc,clh->lhij", pair_normed, bias_weight, preferred_element_type=jnp.float32)
+        .astype(jnp.bfloat16)
+        .reshape(LAYERS, cols, heads, tokens, tokens)
+    )
+    mask = jnp.broadcast_to((token_mask > 0).astype(jnp.float32)[None, :], (8, tokens))
+    bf16, f32 = jnp.bfloat16, jnp.float32
+    dma = pltpu.SemaphoreType.DMA
+    return pl.pallas_call(
+        lambda *refs: fused(rows, cols, *refs),
+        out_shape=jax.ShapeDtypeStruct(single.shape, bf16),
+        in_specs=[pl.BlockSpec(memory_space=pltpu.VMEM)] * 9,
+        out_specs=pl.BlockSpec(memory_space=pltpu.VMEM),
+        scratch_shapes=[
+            pltpu.VMEM((LAYERS, rows, cols, heads, tokens, tokens), bf16),
+            pltpu.VMEM((LAYERS, own, cols, tokens, full), bf16),
+            pltpu.VMEM((cols, LAYERS, width, full), bf16),
+            pltpu.VMEM((own, tokens, full), f32),
+            pltpu.VMEM((cols, tokens + 16, chans), bf16),
+            pltpu.VMEM((samples, tokens, width), bf16),
+            pltpu.VMEM((cols, own, tokens, width), bf16),
+            pltpu.VMEM((rows, 8, tokens), f32),
+            pltpu.VMEM((own, depth, width), bf16),
+            pltpu.VMEM((own, depth, width), bf16),
+            pltpu.VMEM((own, depth, width), bf16),
+            pltpu.VMEM((own, depth, width), f32),
+            pltpu.VMEM((LAYERS, rows, own, tokens, width), bf16),
+            pltpu.VMEM((LAYERS, cols, own, tokens, width), bf16),
+            pltpu.VMEM((cols, own, tokens, width), bf16),
+            dma((2, cols)),
+            dma((2, rows)),
+            dma((2, LAYERS, cols)),
+            dma((2, LAYERS, 2, rows)),
+            dma((2, 3)),
+            dma((2, max(rows, cols))),
+            dma((2, LAYERS, own, 3)),
+            dma((2, LAYERS, cols)),
+            dma((2, max(rows, cols))),
+        ],
+        compiler_params=pltpu.CompilerParams(
+            collective_id=0, has_side_effects=True, vmem_limit_bytes=56 * 1024 * 1024
+        ),
+        name="fused_blocks",
+    )(
+        biases,
+        single,
+        atom_feats,
+        atom_token.reshape(1, slots),
+        atom_count.reshape(1, 1),
+        atom_weight,
+        mask,
+        qkvg_weight,
+        out_weight,
+    )
+
+
 def solution(mesh):
+    rows, cols = mesh.shape["row"], mesh.shape["col"]
     placed = (
         P(None, ("parts", "row"), "col"),
         P(("parts", "row"), "col", None),
@@ -141,8 +747,16 @@
         P(None, None, "col", None),
         P(None, "col", None),
     )
+
+    def body(single, *rest):
+        pairs = rest[0].shape
+        square = rows == cols == 4 and single.shape[0] % rows == 0 and pairs[0] == pairs[1]
+        if square and single.shape[2] % HEAD_DIM == 0:
+            return per_device_fused(rows, cols, single, *rest)
+        return per_device(single, *rest)
+
     return jax.shard_map(
-        per_device,
+        body,
         mesh=mesh,
         in_specs=placed,
         out_specs=P(None, ("parts", "row"), "col"),

time: 298 us -> 160 us (0.54)
  waiting for transfers between devices: 168 us -> 0 us
  Pallas kernels: 0 us -> 139 us
  matrix products: 39.9 us -> 5.97 us
  blocking collectives: 30.7 us -> 0 us
  other arithmetic: 27.3 us -> 8.24 us
  between operations: 14.6 us -> 0.74 us
  starting transfers between devices: 5.05 us -> 0 us
  local copies, waits for them, and re-layouts: 9.73 us -> 5.8 us
    all_gather x8 -> x0, waiting for transfers between devices: 167 us -> none  [the longest x2 57.1 us: per_device(): lax.all_gather(value_rows, 'row', axis=1, tiled=True)]
    pallas_call x0 -> x1, Pallas kernels: none -> 139 us  [per_device_fused(): pl.pallas_call(lambda *refs: fused(rows, cols, *refs), out_shape=jax.Shap...]
    dot_general x11 -> x1, matrix products: 39.9 us -> 5.97 us  [per_device_fused(): jnp.einsum('ijc,clh->lhij', pair_normed, bias_weight, preferred_element_t...]
    psum x1 -> x0, blocking collectives: 11 us -> none  [per_device(): lax.psum(atom_sums.astype(jnp.bfloat16), 'col').astype(jnp.float32)]
    all_to_all x1 -> x0, blocking collectives: 10.3 us -> none  [per_device(): lax.all_to_all(biases[layer_idx], 'col', split_axis=0, concat_axis=2, til...]
    all_gather x1 -> x0, blocking collectives: 9.47 us -> none  [per_device(): lax.all_gather(live_keys, 'row', axis=1, tiled=True)]
    convert_element_type x5 -> x1, other arithmetic: 6.37 us -> 0.01 us  [per_device_fused(): (token_mask > 0).astype(jnp.float32)[None, :]]
    reduce_sum x3 -> x0, other arithmetic: 5.44 us -> none  [the longest x2 4.65 us: attend(): summed_new = jnp.sum(exponent, axis=-1)]
  transfers between devices with their start and end apart: 9 -> 0, of which waited for: 8 -> 0; matrix products, arithmetic and copies ran while one was open for 9% -> 0% of each run, Pallas kernels for 0% -> 0%
where the time goes in v1:
time: 160 us
  Pallas kernels  139 us (87%)
  other arithmetic  8.24 us (5%)
  matrix products  5.97 us (4%)
  local copies, waits for them, and re-layouts  5.8 us (4%)
    pallas_call x1, Pallas kernels, per_device_fused(): pl.pallas_call(lambda *refs: fused(rows, cols, *refs), out_shape=jax.Shap...  139 us
    dot_general x1, matrix products, per_device_fused(): jnp.einsum('ijc,clh->lhij', pair_normed, bias_weight, preferred_element_t...  5.97 us
    reduce_sum x1, other arithmetic, layer_norm(): variance = jnp.mean(centered * centered, axis=-1, keepdims=True)  4.71 us
    reduce_sum x1, other arithmetic, layer_norm(): average = jnp.mean(values, axis=-1, keepdims=True)  3.51 us

profile of v1, /device:TPU:7, one launch (start us, length us, event | category | flops | bytes accessed | tf_op | source)
XLA Modules:
  0.0 159.9 jit_solution(7893748445514702481)
XLA Ops:
  0.0 0.0 copy-start
  0.0 0.0 copy-start.1
  0.0 3.5 %convert_reduce_fusion = f32[128,128]{1,0:T(8,128)S(1)} fusion(bf16[128,128,128]{2,1,0:T(8,128)(2,1)} %param.11), kind=kLoop, calls=%fused_computation.1 | loop fusion | flops 4177920 | bytes 4259840 | tf_op jit(solution)/shard_map/reduce_sum | solution.py:20
  3.5 0.0 copy-done.1
  3.5 4.7 %fusion.2 = f32[128,128]{1,0:T(8,128)S(1)} fusion(bf16[128,128,128]{2,1,0:T(8,128)(2,1)S(1)} %copy-done.1, f32[128,128]{1,0:T(8,128)S(1)} %broadcast_multiply_fusion), kind=kLoop, calls=%fused_computation.4 | loop fusion | flops 8372224 | bytes 4325376 | tf_op jit(solution)/shard_map/reduce_sum | solution.py:22
  8.3 0.0 copy-done
  8.3 0.0 copy-start.2
  8.3 0.0 copy-start.3
  8.3 0.0 copy-start.4
  8.3 6.0 %fusion.10 = bf16[2,16,128,128]{3,1,0,2:T(8,128)(2,1)S(1)} fusion(bf16[128,128,128]{2,1,0:T(8,128)(2,1)S(1)} %copy-done.1, f32[128,128]{1,0:T(8,128)S(1)} %add_rsqrt_fusion, f32[128,128]{1,0:T(8,128)S(1)} %broadcast_multiply_fusion, bf16[128,2,16]{0,2,1:T(8,128)(2,1)S(1)} %copy-done), kind=kOutput, calls=%fused_computation.9 | convolution fusion | flops 143130624 | bytes 5382144 | tf_op jit(solution)/shard_map/ijc,clh->lhij/dot_general | solution.py:681
  14.3 1.4 copy.11
  15.7 0.0 copy-done.2
  15.7 1.0 copy.12.refs_1_
  16.8 0.0 copy-done.3
  16.8 0.7 copy.13.refs_5_
  17.5 0.0 copy-done.4
  17.5 0.6 broadcast_in_dim.2.refs_6_
  18.8 139.2 %fused_blocks.1 = bf16[8,128,192]{2,1,0:T(8,128)(2,1)} custom-call(bf16[2,4,4,128,128]{4,3,2,1,0:T(8,128)(2,1)} %bitcast.18, bf16[8,128,192]{2,1,0:T(8,128)(2,1)} %copy.12.refs_1_, bf16[256,128]{1,0:T(8,128)(2,1)} %refs_2_.1, s32[1,256]{1,0:T(1,128)} %bitcast.19, s32[1,1]{1,0:T(1,128)} %bitcast.17.refs_4_, bf16[128,192]{1,0:T(8,128)(2,1)} %copy.13.refs_5_, ...), custom_call_target="tpu_custom_call" | custom-call | tf_op jit(solution)/shard_map/fused_blocks/pallas_call | solution.py:688
  157.9 2.0 %copy.14 = bf16[8,128,192]{1,2,0:T(8,128)(2,1)} copy(bf16[8,128,192]{2,1,0:T(8,128)(2,1)} %fused_blocks.1) | data formatting | bytes 786432 | tf_op jit(solution)/shard_map/fused_blocks/pallas_call | solution.py:688
  (3 shorter events, 0.0 us)
Async XLA Ops:
  0.0 8.3 %copy-start = (bf16[128,2,16]{0,2,1:T(8,128)(2,1)S(1)}, bf16[128,2,16]{0,2,1:T(8,128)(2,1)}, u32[]{:S(2)}) copy-start(bf16[128,2,16]{0,2,1:T(8,128)(2,1)} %param.17) | copy-start | bytes 24580
  0.0 3.5 %copy-start.1 = (bf16[128,128,128]{2,1,0:T(8,128)(2,1)S(1)}, bf16[128,128,128]{2,1,0:T(8,128)(2,1)}, u32[]{:S(2)}) copy-start(bf16[128,128,128]{2,1,0:T(8,128)(2,1)} %param.11) | copy-start | bytes 12582916
  8.3 7.4 %copy-start.2 = (bf16[8,128,192]{1,2,0:T(8,128)(2,1)S(1)}, bf16[8,128,192]{1,2,0:T(8,128)(2,1)}, u32[]{:S(2)}) copy-start(bf16[8,128,192]{1,2,0:T(8,128)(2,1)} %param.10) | copy-start | bytes 1179652
  8.3 8.4 %copy-start.3 = (bf16[128,192]{0,1:T(8,128)(2,1)S(1)}, bf16[128,192]{0,1:T(8,128)(2,1)}, u32[]{:S(2)}) copy-start(bf16[128,192]{0,1:T(8,128)(2,1)} %param.16) | copy-start | bytes 147460
  8.3 9.2 %copy-start.4 = (s32[128]{0:T(128)S(1)}, s32[128]{0:T(128)}, u32[]{:S(2)}) copy-start(s32[128]{0:T(128)} %param.12) | copy-start | bytes 1540

commit v2 on v1

--- a/solution.py
+++ b/solution.py
@@ -367,15 +367,30 @@
 
     bias_exchange_wait(0)
     ring_send(0, 0)
-    bias_exchange(1)
-
-    for kind, to in ((0, sibling), (1, across)):
-        desc = remote(
-            out_w, out_full.at[c], out_w_sems.at[0, kind], out_w_sems.at[1, kind], r, to
-        )
-        desc.start()
-        sent.append(desc)
-    out_full[c] = out_w[...]
+
+    def out_w_send(l):
+        for kind, to in ((0, sibling), (1, across)):
+            desc = remote(
+                out_w.at[l],
+                out_full.at[c, l],
+                out_w_sems.at[0, l, kind],
+                out_w_sems.at[1, l, kind],
+                r,
+                to,
+            )
+            desc.start()
+            sent.append(desc)
+        out_full[c, l] = out_w[l]
+
+    def out_w_arrived(l, kind, block):
+        remote(
+            out_w.at[l],
+            out_full.at[block, l],
+            out_w_sems.at[0, l, kind],
+            out_w_sems.at[1, l, kind],
+            r,
+            sibling,
+        ).wait_recv()
 
     for f in range(cols):
 
@@ -519,27 +534,15 @@
         send_normed(0, s, here)
 
     for l in range(LAYERS):
-        if l > 0:
-            advance(l, 0)
         for s in range(own):
             forward_normed(l, s)
+            if s == 0:
+                advance(l, 0)
+        if l + 1 < LAYERS:
+            bias_exchange(l + 1)
+        out_w_send(l)
         for s in range(own):
             project(l, s)
-        if l == 0:
-            advance(l, 0)
-            remote(
-                out_w, out_full.at[across], out_w_sems.at[0, 1], out_w_sems.at[1, 1], r, across
-            ).wait_recv()
-            desc = remote(
-                out_full.at[across],
-                out_full.at[across],
-                out_w_sems.at[0, 2],
-                out_w_sems.at[1, 2],
-                r,
-                sibling,
-            )
-            desc.start()
-            sent.append(desc)
 
         def ring_round(t, carry, l=l):
             def side(k, inner):
@@ -557,22 +560,29 @@
             def _():
                 advance(l, t)
 
-            return carry
-
-        lax.fori_loop(0, rows, ring_round, 0)
-        if l + 1 < LAYERS:
-            bias_exchange_wait(l + 1)
-            ring_send(l + 1, 0)
-        if l == 0:
-            for kind, block in ((0, sibling), (2, far)):
+            @pl.when(t == rows - 2)
+            def _():
+                if l + 1 < LAYERS:
+                    bias_exchange_wait(l + 1)
+                    ring_send(l + 1, 0)
+
+            @pl.when(t == 1)
+            def _():
+                out_w_arrived(l, 1, across)
                 remote(
-                    out_w,
-                    out_full.at[block],
-                    out_w_sems.at[0, kind],
-                    out_w_sems.at[1, kind],
+                    out_full.at[across, l],
+                    out_full.at[across, l],
+                    out_w_sems.at[0, l, 2],
+                    out_w_sems.at[1, l, 2],
                     r,
                     sibling,
-                ).wait_recv()
+                ).start()
+
+            return carry
+
+        lax.fori_loop(0, rows, ring_round, 0)
+        out_w_arrived(l, 0, sibling)
+        out_w_arrived(l, 2, far)
         gated_wait(l)
         for s in range(own):
             joined = jnp.concatenate(
@@ -641,6 +651,14 @@
         ).wait_send()
 
     for l in range(LAYERS):
+        remote(
+            out_full.at[across, l],
+            out_full.at[across, l],
+            out_w_sems.at[0, l, 2],
+            out_w_sems.at[1, l, 2],
+            r,
+            sibling,
+        ).wait_send()
         for step in range(rows - 1):
             ring_sent(l, step)
         for d in range(1, cols):
@@ -710,7 +728,7 @@
             dma((2, rows)),
             dma((2, LAYERS, cols)),
             dma((2, LAYERS, 2, rows)),
-            dma((2, 3)),
+            dma((2, LAYERS, 3)),
             dma((2, max(rows, cols))),
             dma((2, LAYERS, own, 3)),
             dma((2, LAYERS, cols)),

time: 160 us -> 145 us (0.906)
  Pallas kernels: 139 us -> 124 us
    pallas_call x1, Pallas kernels: 139 us -> 124 us  [per_device_fused(): pl.pallas_call(lambda *refs: fused(rows, cols, *refs), out_shape=jax.Shap...]
where the time goes in v2:
time: 145 us
  Pallas kernels  124 us (86%)
  other arithmetic  8.24 us (6%)
  matrix products  5.97 us (4%)
  local copies, waits for them, and re-layouts  5.8 us (4%)
    pallas_call x1, Pallas kernels, per_device_fused(): pl.pallas_call(lambda *refs: fused(rows, cols, *refs), out_shape=jax.Shap...  124 us
    dot_general x1, matrix products, per_device_fused(): jnp.einsum('ijc,clh->lhij', pair_normed, bias_weight, preferred_element_t...  5.97 us
    reduce_sum x1, other arithmetic, layer_norm(): variance = jnp.mean(centered * centered, axis=-1, keepdims=True)  4.71 us
    reduce_sum x1, other arithmetic, layer_norm(): average = jnp.mean(values, axis=-1, keepdims=True)  3.51 us

profile of v2, /device:TPU:7, one launch (start us, length us, event | category | flops | bytes accessed | tf_op | source)
XLA Modules:
  0.0 144.7 jit_solution(18064280831393204478)
XLA Ops:
  0.0 0.0 copy-start
  0.0 0.0 copy-start.1
  0.0 3.5 %convert_reduce_fusion = f32[128,128]{1,0:T(8,128)S(1)} fusion(bf16[128,128,128]{2,1,0:T(8,128)(2,1)} %param.11), kind=kLoop, calls=%fused_computation.1 | loop fusion | flops 4177920 | bytes 4259840 | tf_op jit(solution)/shard_map/reduce_sum | solution.py:20
  3.5 0.0 copy-done.1
  3.5 4.7 %fusion.2 = f32[128,128]{1,0:T(8,128)S(1)} fusion(bf16[128,128,128]{2,1,0:T(8,128)(2,1)S(1)} %copy-done.1, f32[128,128]{1,0:T(8,128)S(1)} %broadcast_multiply_fusion), kind=kLoop, calls=%fused_computation.4 | loop fusion | flops 8372224 | bytes 4325376 | tf_op jit(solution)/shard_map/reduce_sum | solution.py:22
  8.3 0.0 copy-done
  8.3 0.0 copy-start.2
  8.3 0.0 copy-start.3
  8.3 0.0 copy-start.4
  8.3 6.0 %fusion.10 = bf16[2,16,128,128]{3,1,0,2:T(8,128)(2,1)S(1)} fusion(bf16[128,128,128]{2,1,0:T(8,128)(2,1)S(1)} %copy-done.1, f32[128,128]{1,0:T(8,128)S(1)} %add_rsqrt_fusion, f32[128,128]{1,0:T(8,128)S(1)} %broadcast_multiply_fusion, bf16[128,2,16]{0,2,1:T(8,128)(2,1)S(1)} %copy-done), kind=kOutput, calls=%fused_computation.9 | convolution fusion | flops 143130624 | bytes 5382144 | tf_op jit(solution)/shard_map/ijc,clh->lhij/dot_general | solution.py:699
  14.3 1.4 copy.11
  15.7 0.0 copy-done.2
  15.7 1.0 copy.12.refs_1_
  16.8 0.0 copy-done.3
  16.8 0.7 copy.13.refs_5_
  17.5 0.0 copy-done.4
  17.5 0.6 broadcast_in_dim.2.refs_6_
  18.8 123.9 %fused_blocks.1 = bf16[8,128,192]{2,1,0:T(8,128)(2,1)} custom-call(bf16[2,4,4,128,128]{4,3,2,1,0:T(8,128)(2,1)} %bitcast.18, bf16[8,128,192]{2,1,0:T(8,128)(2,1)} %copy.12.refs_1_, bf16[256,128]{1,0:T(8,128)(2,1)} %refs_2_.1, s32[1,256]{1,0:T(1,128)} %bitcast.19, s32[1,1]{1,0:T(1,128)} %bitcast.17.refs_4_, bf16[128,192]{1,0:T(8,128)(2,1)} %copy.13.refs_5_, ...), custom_call_target="tpu_custom_call" | custom-call | tf_op jit(solution)/shard_map/fused_blocks/pallas_call | solution.py:706
  142.7 2.0 %copy.14 = bf16[8,128,192]{1,2,0:T(8,128)(2,1)} copy(bf16[8,128,192]{2,1,0:T(8,128)(2,1)} %fused_blocks.1) | data formatting | bytes 786432 | tf_op jit(solution)/shard_map/fused_blocks/pallas_call | solution.py:706
  (3 shorter events, 0.0 us)
Async XLA Ops:
  0.0 8.3 %copy-start = (bf16[128,2,16]{0,2,1:T(8,128)(2,1)S(1)}, bf16[128,2,16]{0,2,1:T(8,128)(2,1)}, u32[]{:S(2)}) copy-start(bf16[128,2,16]{0,2,1:T(8,128)(2,1)} %param.17) | copy-start | bytes 24580
  0.0 3.5 %copy-start.1 = (bf16[128,128,128]{2,1,0:T(8,128)(2,1)S(1)}, bf16[128,128,128]{2,1,0:T(8,128)(2,1)}, u32[]{:S(2)}) copy-start(bf16[128,128,128]{2,1,0:T(8,128)(2,1)} %param.11) | copy-start | bytes 12582916
  8.3 7.4 %copy-start.2 = (bf16[8,128,192]{1,2,0:T(8,128)(2,1)S(1)}, bf16[8,128,192]{1,2,0:T(8,128)(2,1)}, u32[]{:S(2)}) copy-start(bf16[8,128,192]{1,2,0:T(8,128)(2,1)} %param.10) | copy-start | bytes 1179652
  8.3 8.4 %copy-start.3 = (bf16[128,192]{0,1:T(8,128)(2,1)S(1)}, bf16[128,192]{0,1:T(8,128)(2,1)}, u32[]{:S(2)}) copy-start(bf16[128,192]{0,1:T(8,128)(2,1)} %param.16) | copy-start | bytes 147460
  8.3 9.2 %copy-start.4 = (s32[128]{0:T(128)S(1)}, s32[128]{0:T(128)}, u32[]{:S(2)}) copy-start(s32[128]{0:T(128)} %param.12) | copy-start | bytes 1540

commit v3 on v2

--- a/solution.py
+++ b/solution.py
@@ -186,10 +186,9 @@
     r = lax.axis_index("row")
     c = lax.axis_index("col")
     own = single.shape[0] // rows
-    tokens = single.shape[1]
-    width = single.shape[2]
+    tokens = single.shape[2]
+    width = single.shape[1]
     heads = width // HEAD_DIM
-    depth = rows * tokens
     sibling = c + 1 - 2 * lax.rem(c, 2)
     across = lax.rem(c + 2, cols)
     far = lax.rem(sibling + 2, cols)
@@ -332,19 +331,14 @@
         remote(
             parts_buf.at[frm], parts_buf.at[frm], part_sems.at[0, d], part_sems.at[1, d], r, frm
         ).wait_recv()
-    total = jnp.zeros((tokens, width), jnp.float32)
+    total = jnp.zeros((width, tokens), jnp.float32)
     count_row = jnp.zeros((1, tokens), jnp.float32)
     for k in range(cols):
-        total = total + jnp.dot(
-            parts_buf[k, 0:tokens], atom_weight[...], preferred_element_type=jnp.float32
+        total = total + lax.dot_general(
+            atom_weight[...], parts_buf[k, 0:tokens], NT, preferred_element_type=jnp.float32
         )
         count_row = count_row + parts_buf[k, tokens : tokens + 16].astype(jnp.float32)[0:1]
-    square = (
-        lax.broadcasted_iota(jnp.int32, (tokens, tokens), 0)
-        == lax.broadcasted_iota(jnp.int32, (tokens, tokens), 1)
-    )
-    count_col = jnp.sum(jnp.where(square, count_row, 0.0), axis=1, keepdims=True)
-    pooled = total / count_col
+    pooled = total / count_row
     for s in range(single.shape[0]):
         stream_send[s] = (single[s].astype(jnp.float32) + pooled).astype(jnp.bfloat16)
     for d in range(rows):
@@ -406,9 +400,9 @@
             ).wait_recv()
 
     def send_normed(l, s, here):
-        average = jnp.mean(here, axis=-1, keepdims=True)
+        average = jnp.mean(here, axis=0, keepdims=True)
         centered = here - average
-        variance = jnp.mean(centered * centered, axis=-1, keepdims=True)
+        variance = jnp.mean(centered * centered, axis=0, keepdims=True)
         normed[l, s, c] = (centered * lax.rsqrt(variance + EPS)).astype(jnp.bfloat16)
         for kind, to in ((0, sibling), (1, across)):
             desc = remote(
@@ -452,30 +446,35 @@
                 r,
                 sibling,
             ).wait_recv()
-        here = normed[l, s].reshape(depth, normed.shape[-1])
-        for f, target in enumerate((queries, keys, values)):
-            target[s] = lax.dot_general(
-                here, qkvg[l, f], NT, preferred_element_type=jnp.float32
-            ).astype(jnp.bfloat16)
-        gates[s] = jax.nn.sigmoid(
-            lax.dot_general(here, qkvg[l, 3], NT, preferred_element_type=jnp.float32)
-        )
+        here = jnp.concatenate([normed[l, s, k] for k in range(cols)], axis=1)
+
+        def rows_of(f):
+            return jnp.dot(qkvg[l, f], here, preferred_element_type=jnp.float32)
+
+        keys[s] = rows_of(1).astype(jnp.bfloat16)
+        values[s] = rows_of(2).astype(jnp.bfloat16)
+        query = rows_of(0)
+        gating = jax.nn.sigmoid(rows_of(3))
+        for k in range(cols):
+            at = slice(k * tokens, (k + 1) * tokens)
+            queries[s, k] = query[:, at].T.astype(jnp.bfloat16)
+            gates[s, k] = gating[:, at]
 
     score_scale = 1.0 / math.sqrt(HEAD_DIM)
 
     def attend(l, block):
         live = jnp.concatenate([mask_buf[k][0:1] for k in range(rows)], axis=1) > 0
-        lane_head = lax.broadcasted_iota(jnp.int32, (tokens, width), 1)
+        square = lax.broadcasted_iota(jnp.int32, (tokens, tokens), 0) == lax.broadcasted_iota(
+            jnp.int32, (tokens, tokens), 1
+        )
 
         def one_sample(s, carry):
-            rows_at = pl.ds(pl.multiple_of(block * tokens, tokens), tokens)
-            query = queries[s, rows_at, :]
-            attended = jnp.zeros((tokens, width), jnp.float32)
             for h in range(heads):
-                mine = (lane_head >= h * HEAD_DIM) & (lane_head < (h + 1) * HEAD_DIM)
-                masked = jnp.where(mine, query.astype(jnp.float32), 0.0).astype(jnp.bfloat16)
+                at = slice(h * HEAD_DIM, (h + 1) * HEAD_DIM)
                 scores = (
-                    lax.dot_general(masked, keys[s], NT, preferred_element_type=jnp.float32)
+                    jnp.dot(
+                        queries[s, block, :, at], keys[s, at], preferred_element_type=jnp.float32
+                    )
                     * score_scale
                 )
                 head_bias = jnp.concatenate([spread[l, block, k, h] for k in range(cols)], axis=1)
@@ -484,11 +483,15 @@
                 highest = jnp.max(scores, axis=-1, keepdims=True)
                 exponent = jnp.exp(scores - highest)
                 summed = jnp.sum(exponent, axis=-1, keepdims=True)
-                mixed = jnp.dot(
-                    exponent.astype(jnp.bfloat16), values[s], preferred_element_type=jnp.float32
+                mixed = lax.dot_general(
+                    values[s, at],
+                    exponent.astype(jnp.bfloat16),
+                    NT,
+                    preferred_element_type=jnp.float32,
                 )
-                attended = jnp.where(mine, mixed * (1.0 / summed), attended)
-            gated_send[l, block, s] = (gates[s, rows_at, :] * attended).astype(jnp.bfloat16)
+                summed_row = jnp.sum(jnp.where(square, summed, 0.0), axis=0, keepdims=True)
+                attended = mixed * (1.0 / summed_row)
+                gated_send[l, block, s, at] = (gates[s, block, at] * attended).astype(jnp.bfloat16)
             return carry
 
         lax.fori_loop(0, own, one_sample, 0)
@@ -529,7 +532,7 @@
         ).wait_recv()
 
     for s in range(own):
-        here = jnp.concatenate([stream_recv[f, s].astype(jnp.float32) for f in range(cols)], axis=1)
+        here = jnp.concatenate([stream_recv[f, s].astype(jnp.float32) for f in range(cols)], axis=0)
         stream[s] = here
         send_normed(0, s, here)
 
@@ -584,14 +587,17 @@
         out_w_arrived(l, 0, sibling)
         out_w_arrived(l, 2, far)
         gated_wait(l)
+        joined = jnp.concatenate(
+            [
+                jnp.concatenate([gated_recv[l, k, s] for k in range(cols)], axis=0)
+                for s in range(own)
+            ],
+            axis=1,
+        )
+        weight = jnp.concatenate([out_full[k, l] for k in range(cols)], axis=0)
+        update = jnp.dot(weight, joined, preferred_element_type=jnp.float32)
         for s in range(own):
-            joined = jnp.concatenate(
-                [gated_recv[l, k, s].astype(jnp.float32) for k in range(cols)], axis=1
-            ).astype(jnp.bfloat16)
-            weight = jnp.concatenate([out_full[k, l] for k in range(cols)], axis=0)
-            here = stream[s] + lax.dot_general(
-                joined, weight, NT, preferred_element_type=jnp.float32
-            )
+            here = stream[s] + update[:, s * tokens : (s + 1) * tokens]
             rounded = here.astype(jnp.bfloat16)
             here = rounded.astype(jnp.float32)
             if l + 1 < LAYERS:
@@ -599,7 +605,7 @@
                 send_normed(l + 1, s, here)
             else:
                 for f in range(cols):
-                    final_send[f, s] = here[:, f * width : (f + 1) * width].astype(jnp.bfloat16)
+                    final_send[f, s] = here[f * width : (f + 1) * width].astype(jnp.bfloat16)
 
     place = pl.ds(r * own, own)
 
@@ -688,6 +694,7 @@
     out_weight,
 ):
     samples, tokens, width = single.shape
+    single = single.transpose(0, 2, 1)
     own = samples // rows
     depth = rows * tokens
     heads = width // HEAD_DIM
@@ -703,27 +710,27 @@
     mask = jnp.broadcast_to((token_mask > 0).astype(jnp.float32)[None, :], (8, tokens))
     bf16, f32 = jnp.bfloat16, jnp.float32
     dma = pltpu.SemaphoreType.DMA
-    return pl.pallas_call(
+    updated = pl.pallas_call(
         lambda *refs: fused(rows, cols, *refs),
         out_shape=jax.ShapeDtypeStruct(single.shape, bf16),
         in_specs=[pl.BlockSpec(memory_space=pltpu.VMEM)] * 9,
         out_specs=pl.BlockSpec(memory_space=pltpu.VMEM),
         scratch_shapes=[
             pltpu.VMEM((LAYERS, rows, cols, heads, tokens, tokens), bf16),
-            pltpu.VMEM((LAYERS, own, cols, tokens, full), bf16),
+            pltpu.VMEM((LAYERS, own, cols, full, tokens), bf16),
             pltpu.VMEM((cols, LAYERS, width, full), bf16),
-            pltpu.VMEM((own, tokens, full), f32),
+            pltpu.VMEM((own, full, tokens), f32),
             pltpu.VMEM((cols, tokens + 16, chans), bf16),
-            pltpu.VMEM((samples, tokens, width), bf16),
-            pltpu.VMEM((cols, own, tokens, width), bf16),
+            pltpu.VMEM((samples, width, tokens), bf16),
+            pltpu.VMEM((cols, own, width, tokens), bf16),
             pltpu.VMEM((rows, 8, tokens), f32),
-            pltpu.VMEM((own, depth, width), bf16),
-            pltpu.VMEM((own, depth, width), bf16),
-            pltpu.VMEM((own, depth, width), bf16),
-            pltpu.VMEM((own, depth, width), f32),
-            pltpu.VMEM((LAYERS, rows, own, tokens, width), bf16),
-            pltpu.VMEM((LAYERS, cols, own, tokens, width), bf16),
-            pltpu.VMEM((cols, own, tokens, width), bf16),
+            pltpu.VMEM((own, rows, tokens, width), bf16),
+            pltpu.VMEM((own, width, depth), bf16),
+            pltpu.VMEM((own, width, depth), bf16),
+            pltpu.VMEM((own, rows, width, tokens), f32),
+            pltpu.VMEM((LAYERS, rows, own, width, tokens), bf16),
+            pltpu.VMEM((LAYERS, cols, own, width, tokens), bf16),
+            pltpu.VMEM((cols, own, width, tokens), bf16),
             dma((2, cols)),
             dma((2, rows)),
             dma((2, LAYERS, cols)),
@@ -744,11 +751,12 @@
         atom_feats,
         atom_token.reshape(1, slots),
         atom_count.reshape(1, 1),
-        atom_weight,
+        atom_weight.T,
         mask,
         qkvg_weight,
         out_weight,
     )
+    return updated.transpose(0, 2, 1)
 
 
 def solution(mesh):

time: 145 us -> 135 us (0.931)
  Pallas kernels: 124 us -> 116 us
  local copies, waits for them, and re-layouts: 5.8 us -> 3.78 us
    pallas_call x1, Pallas kernels: 124 us -> 116 us  [per_device_fused(): pl.pallas_call(lambda *refs: fused(rows, cols, *refs), out_shape=jax.Shap...]
    pallas_call x1 -> x0, local copies, waits for them, and re-layouts: 1.99 us -> none  [per_device_fused(): pl.pallas_call(lambda *refs: fused(rows, cols, *refs), out_shape=jax.Shap...]
where the time goes in v3:
time: 135 us
  Pallas kernels  116 us (86%)
  other arithmetic  8.31 us (6%)
  matrix products  5.97 us (4%)
  local copies, waits for them, and re-layouts  3.78 us (3%)
    pallas_call x1, Pallas kernels, per_device_fused(): pl.pallas_call(lambda *refs: fused(rows, cols, *refs), out_shape=jax.Shap...  116 us
    dot_general x1, matrix products, per_device_fused(): jnp.einsum('ijc,clh->lhij', pair_normed, bias_weight, preferred_element_t...  5.97 us
    reduce_sum x1, other arithmetic, layer_norm(): variance = jnp.mean(centered * centered, axis=-1, keepdims=True)  4.77 us
    reduce_sum x1, other arithmetic, layer_norm(): average = jnp.mean(values, axis=-1, keepdims=True)  3.51 us

profile of v3, /device:TPU:7, one launch (start us, length us, event | category | flops | bytes accessed | tf_op | source)
XLA Modules:
  0.0 135.0 jit_solution(11138040316941977508)
XLA Ops:
  0.0 0.0 copy-start
  0.0 0.0 copy-start.1
  0.0 3.5 %convert_reduce_fusion = f32[128,128]{1,0:T(8,128)S(1)} fusion(bf16[128,128,128]{2,1,0:T(8,128)(2,1)} %param.11), kind=kLoop, calls=%fused_computation.1 | loop fusion | flops 4177920 | bytes 4259840 | tf_op jit(solution)/shard_map/reduce_sum | solution.py:20
  3.5 0.0 copy-done.1
  3.5 4.8 %fusion.2 = f32[128,128]{1,0:T(8,128)S(1)} fusion(bf16[128,128,128]{2,1,0:T(8,128)(2,1)S(1)} %copy-done.1, f32[128,128]{1,0:T(8,128)S(1)} %broadcast_multiply_fusion), kind=kLoop, calls=%fused_computation.4 | loop fusion | flops 8372224 | bytes 4325376 | tf_op jit(solution)/shard_map/reduce_sum | solution.py:22
  8.3 0.0 copy-done
  8.4 0.0 copy-start.2
  8.4 6.0 %fusion.10 = bf16[2,16,128,128]{3,1,0,2:T(8,128)(2,1)S(1)} fusion(bf16[128,128,128]{2,1,0:T(8,128)(2,1)S(1)} %copy-done.1, f32[128,128]{1,0:T(8,128)S(1)} %add_rsqrt_fusion, f32[128,128]{1,0:T(8,128)S(1)} %broadcast_multiply_fusion, bf16[128,2,16]{0,2,1:T(8,128)(2,1)S(1)} %copy-done), kind=kOutput, calls=%fused_computation.9 | convolution fusion | flops 143130624 | bytes 5382144 | tf_op jit(solution)/shard_map/ijc,clh->lhij/dot_general | solution.py:706
  14.3 1.4 %copy.11 = bf16[2,16,128,128]{3,2,1,0:T(8,128)(2,1)} copy(bf16[2,16,128,128]{3,1,0,2:T(8,128)(2,1)S(1)} %fusion.10) | data formatting | bytes 2097152 | tf_op jit(solution)/shard_map/convert_element_type | solution.py:707
  15.7 0.0 copy-done.2
  15.8 0.6 broadcast_in_dim.2.refs_6_
  17.0 116.2 %fused_blocks.1 = bf16[8,192,128]{2,1,0:T(8,128)(2,1)} custom-call(bf16[2,4,4,128,128]{4,3,2,1,0:T(8,128)(2,1)} %bitcast.21, bf16[8,192,128]{2,1,0:T(8,128)(2,1)} %bitcast.23, bf16[256,128]{1,0:T(8,128)(2,1)} %refs_2_.1, s32[1,256]{1,0:T(1,128)} %bitcast.25, s32[1,1]{1,0:T(1,128)} %bitcast.20.refs_4_, bf16[192,128]{1,0:T(8,128)(2,1)} %bitcast.24, ...), custom_call_target="tpu_custom_call" | custom-call | tf_op jit(solution)/shard_map/fused_blocks/pallas_call | solution.py:713
  133.2 1.8 %copy.15 = bf16[8,128,192]{1,2,0:T(8,128)(2,1)} copy(bf16[8,128,192]{1,2,0:T(8,128)(2,1)} %bitcast.22) | data formatting | bytes 786432
  (3 shorter events, 0.0 us)
Async XLA Ops:
  0.0 8.4 %copy-start = (bf16[128,2,16]{0,2,1:T(8,128)(2,1)S(1)}, bf16[128,2,16]{0,2,1:T(8,128)(2,1)}, u32[]{:S(2)}) copy-start(bf16[128,2,16]{0,2,1:T(8,128)(2,1)} %param.17) | copy-start | bytes 24580
  0.0 3.5 %copy-start.1 = (bf16[128,128,128]{2,1,0:T(8,128)(2,1)S(1)}, bf16[128,128,128]{2,1,0:T(8,128)(2,1)}, u32[]{:S(2)}) copy-start(bf16[128,128,128]{2,1,0:T(8,128)(2,1)} %param.11) | copy-start | bytes 12582916
  8.4 7.4 %copy-start.2 = (s32[128]{0:T(128)S(1)}, s32[128]{0:T(128)}, u32[]{:S(2)}) copy-start(s32[128]{0:T(128)} %param.12) | copy-start | bytes 1540

commit v4 on v3

--- a/solution.py
+++ b/solution.py
@@ -679,6 +679,14 @@
             ).wait_send()
 
 
+def pair_bias(x_ref, w_ref, o_ref):
+    lines, across, chans = x_ref.shape
+    here = x_ref[...].reshape(lines * across, chans).astype(jnp.float32)
+    rounded = layer_norm(here).astype(jnp.bfloat16)
+    biases = lax.dot_general(w_ref[...], rounded, NT, preferred_element_type=jnp.float32)
+    o_ref[...] = biases.reshape(w_ref.shape[0], lines, across).astype(jnp.bfloat16)
+
+
 def per_device_fused(
     rows,
     cols,
@@ -701,12 +709,20 @@
     full = width * cols
     chans = atom_feats.shape[1]
     slots = atom_feats.shape[0]
-    pair_normed = layer_norm(pair_act.astype(jnp.float32)).astype(jnp.bfloat16)
-    biases = (
-        jnp.einsum("ijc,clh->lhij", pair_normed, bias_weight, preferred_element_type=jnp.float32)
-        .astype(jnp.bfloat16)
-        .reshape(LAYERS, cols, heads, tokens, tokens)
-    )
+    lines, pairs = 16, pair_act.shape[2]
+    all_heads = bias_weight.shape[1] * bias_weight.shape[2]
+    biases = pl.pallas_call(
+        pair_bias,
+        grid=(tokens // lines,),
+        in_specs=[
+            pl.BlockSpec((lines, tokens, pairs), lambda i: (i, 0, 0)),
+            pl.BlockSpec((all_heads, pairs), lambda i: (0, 0)),
+        ],
+        out_specs=pl.BlockSpec((all_heads, lines, tokens), lambda i: (0, i, 0)),
+        out_shape=jax.ShapeDtypeStruct((all_heads, tokens, tokens), jnp.bfloat16),
+        name="pair_bias",
+    )(pair_act, bias_weight.reshape(pairs, all_heads).T)
+    biases = biases.reshape(LAYERS, cols, heads, tokens, tokens)
     mask = jnp.broadcast_to((token_mask > 0).astype(jnp.float32)[None, :], (8, tokens))
     bf16, f32 = jnp.bfloat16, jnp.float32
     dma = pltpu.SemaphoreType.DMA
@@ -777,6 +793,7 @@
     def body(single, *rest):
         pairs = rest[0].shape
         square = rows == cols == 4 and single.shape[0] % rows == 0 and pairs[0] == pairs[1]
+        square = square and pairs[0] % 128 == 0
         if square and single.shape[2] % HEAD_DIM == 0:
             return per_device_fused(rows, cols, single, *rest)
         return per_device(single, *rest)

time: 135 us -> 129 us (0.956)
  Pallas kernels: 116 us -> 125 us
  other arithmetic: 8.31 us -> 0.66 us
  matrix products: 5.97 us -> 0 us
  local copies, waits for them, and re-layouts: 3.78 us -> 2.37 us
    pallas_call x0 -> x1, Pallas kernels: none -> 9.15 us  [per_device_fused(): pl.pallas_call(pair_bias, grid=(tokens // lines,), in_specs=[pl.BlockSpec...]
    reduce_sum x2 -> x0, other arithmetic: 8.28 us -> none  [the longest x1 4.77 us: layer_norm(): variance = jnp.mean(centered * centered, axis=-1, keepdims=True)]
    dot_general x1 -> x0, matrix products: 5.97 us -> none  [per_device_fused(): jnp.einsum('ijc,clh->lhij', pair_normed, bias_weight, preferred_element_t...]
    convert_element_type x1 -> x0, local copies, waits for them, and re-layouts: 1.4 us -> none  [per_device_fused(): biases = jnp.einsum('ijc,clh->lhij', pair_normed, bias_weight, preferred_...]
where the time goes in v4:
time: 129 us
  Pallas kernels  125 us (97%)
  local copies, waits for them, and re-layouts  2.37 us (2%)
    pallas_call x1, Pallas kernels, per_device_fused(): pl.pallas_call(lambda *refs: fused(rows, cols, *refs), out_shape=jax.Shap...  116 us
    pallas_call x1, Pallas kernels, per_device_fused(): pl.pallas_call(pair_bias, grid=(tokens // lines,), in_specs=[pl.BlockSpec...  9.15 us

profile of v4, /device:TPU:7, one launch (start us, length us, event | category | flops | bytes accessed | tf_op | source)
XLA Modules:
  0.0 129.0 jit_solution(8262137805577921971)
XLA Ops:
  0.7 0.7 compare_convert_fusion
  1.3 0.6 broadcast_in_dim.2.refs_6_
  1.9 9.1 %pair_bias.1 = bf16[32,128,128]{2,1,0:T(8,128)(2,1)} custom-call(bf16[128,128,128]{2,1,0:T(8,128)(2,1)} %x_ref.1, bf16[32,128]{1,0:T(8,128)(2,1)} %bitcast.14), custom_call_target="tpu_custom_call" | custom-call | tf_op jit(solution)/shard_map/pair_bias/pallas_call | solution.py:714
  11.1 116.2 %fused_blocks.1 = bf16[8,192,128]{2,1,0:T(8,128)(2,1)} custom-call(bf16[2,4,4,128,128]{4,3,2,1,0:T(8,128)(2,1)} %bitcast.10, bf16[8,192,128]{2,1,0:T(8,128)(2,1)} %bitcast.12, bf16[256,128]{1,0:T(8,128)(2,1)} %refs_2_.1, s32[1,256]{1,0:T(1,128)} %bitcast.15, s32[1,1]{1,0:T(1,128)} %bitcast.9.refs_4_, bf16[192,128]{1,0:T(8,128)(2,1)} %bitcast.13, ...), custom_call_target="tpu_custom_call" | custom-call | tf_op jit(solution)/shard_map/fused_blocks/pallas_call | solution.py:729
  127.2 1.8 %copy.13 = bf16[8,128,192]{1,2,0:T(8,128)(2,1)} copy(bf16[8,128,192]{1,2,0:T(8,128)(2,1)} %bitcast.11) | data formatting | bytes 786432
